TPU v7x, 256 devices: a whole 4x4x8 slice. The times are simulated.
256 devices in a mesh: rep: 2 (over z_hi), fsdp: 32 (over y, x, core), tp: 4 (over z_lo).
Axes of the slice: x: 4, y: 4, z: 8 (z_hi: 2, z_lo: 4; z = z_hi * 4 + z_lo), core: 2. Of those that a mesh axis runs over, the one named last changes fastest.
Arguments:
- delta_out: float32 [2, 8, 1792, 1792], P('rep', None, 'tp', 'fsdp'), may hold values from -6 to 6
- delta_down: float32 [2, 8, 4864, 1792], P('rep', None, 'tp', 'fsdp'), may hold values from -6 to 6
- basis: float32 [1792, 64], replicated, may hold values from -0.125 to 0.125
- anchor_out: float32 [8, 4, 448, 1792], P('rep', 'tp', 'fsdp'), may hold values from -6 to 6
- anchor_down: float32 [8, 4, 1216, 1792], P('rep', 'tp', 'fsdp'), may hold values from -6 to 6
- moment_out: float32 [8, 4, 448, 1792], P('rep', 'tp', 'fsdp'), may hold values from -3 to 3
- moment_down: float32 [8, 4, 1216, 1792], P('rep', 'tp', 'fsdp'), may hold values from -3 to 3
Outputs:
- weights_out: bfloat16 [8, 1792, 1792], P(None, 'tp', 'fsdp')
- weights_down: bfloat16 [8, 4864, 1792], P(None, 'tp', 'fsdp')
- anchor_out_new: float32 [8, 4, 448, 1792], P('rep', 'tp', 'fsdp')
- anchor_down_new: float32 [8, 4, 1216, 1792], P('rep', 'tp', 'fsdp')
- moment_out_new: float32 [8, 4, 448, 1792], P('rep', 'tp', 'fsdp')
- moment_down_new: float32 [8, 4, 1216, 1792], P('rep', 'tp', 'fsdp')
All inputs are finite; a program needn't handle non-finite values.
Results may differ from a plain program's by a relative error of at most 0.0055.
Values may be sent and summed in bfloat16 or wider, within the bound.
A program may use at most 64 MiB of HBM per device.

v0:
```python
import jax
import jax.numpy as jnp
from jax import lax
from jax.sharding import PartitionSpec as P

outer_rate = 0.7
nesterov_decay = 0.9


def owner_update(summed, basis, anchor, moment, groups):
    coef = summed / groups
    grad = jnp.einsum("lik,jk->lij", coef, basis, precision=lax.Precision.HIGHEST)
    previous = anchor[:, 0]
    velocity = moment[:, 0]
    moment_new = nesterov_decay * velocity + grad
    anchor_new = previous - outer_rate * (grad + nesterov_decay * moment_new)
    return (anchor_new, moment_new)


def per_device(delta_out, delta_down, basis, anchor_out, anchor_down, moment_out, moment_down):
    groups = lax.axis_size("rep")
    piece_cols = delta_out.shape[3]
    shard_index = lax.axis_index("fsdp")
    basis_rows = lax.dynamic_slice_in_dim(basis, shard_index * piece_cols, piece_cols, 0)
    partial_out = jnp.einsum(
        "lij,jk->lik", delta_out[0], basis_rows, precision=lax.Precision.HIGHEST
    )
    partial_down = jnp.einsum(
        "lij,jk->lik", delta_down[0], basis_rows, precision=lax.Precision.HIGHEST
    )
    layer_sums = (
        lax.psum_scatter(
            partial_out.astype(jnp.bfloat16), "rep", scatter_dimension=0, tiled=True
        ).astype(jnp.float32),
        lax.psum_scatter(
            partial_down.astype(jnp.bfloat16), "rep", scatter_dimension=0, tiled=True
        ).astype(jnp.float32),
    )
    summed_out, summed_down = (
        lax.psum_scatter(
            layer_sums[0].astype(jnp.bfloat16), "fsdp", scatter_dimension=1, tiled=True
        ).astype(jnp.float32),
        lax.psum_scatter(
            layer_sums[1].astype(jnp.bfloat16), "fsdp", scatter_dimension=1, tiled=True
        ).astype(jnp.float32),
    )
    anchor_out_new, moment_out_new = owner_update(summed_out, basis, anchor_out, moment_out, groups)
    anchor_down_new, moment_down_new = owner_update(
        summed_down, basis, anchor_down, moment_down, groups
    )
    rounded_out = anchor_out_new.astype(jnp.bfloat16)
    rounded_down = anchor_down_new.astype(jnp.bfloat16)
    placed_out, placed_down = (
        lax.all_to_all(rounded_out, "fsdp", split_axis=2, concat_axis=1, tiled=True),
        lax.all_to_all(rounded_down, "fsdp", split_axis=2, concat_axis=1, tiled=True),
    )
    weights_out, weights_down = (
        lax.all_gather(placed_out, "rep", axis=0, tiled=True),
        lax.all_gather(placed_down, "rep", axis=0, tiled=True),
    )
    return (
        weights_out,
        weights_down,
        anchor_out_new[:, None],
        anchor_down_new[:, None],
        moment_out_new[:, None],
        moment_down_new[:, None],
    )


def solution(mesh):
    return jax.shard_map(
        per_device,
        mesh=mesh,
        in_specs=(
            P("rep", None, "tp", "fsdp"),
            P("rep", None, "tp", "fsdp"),
            P(),
            P("rep", "tp", "fsdp", None),
            P("rep", "tp", "fsdp", None),
            P("rep", "tp", "fsdp", None),
            P("rep", "tp", "fsdp", None),
        ),
        out_specs=(
            P(None, "tp", "fsdp"),
            P(None, "tp", "fsdp"),
            P("rep", "tp", "fsdp", None),
            P("rep", "tp", "fsdp", None),
            P("rep", "tp", "fsdp", None),
            P("rep", "tp", "fsdp", None),
        ),
        check_vma=False,
    )
```

profile of v0, /device:TPU:32, one launch (start us, length us, event | category | flops | bytes accessed | tf_op | source)
XLA Modules:
  0.0 316.6 jit_solution(11942777162929042482)
XLA Ops:
  7.2 0.0 copy-start
  7.2 0.0 reduce-scatter.3.cloned.1.call-start
  7.2 3.2 %fusion.2 = bf16[8,448,64]{1,2,0:T(8,128)(2,1)} fusion(f32[1,8,448,56]{2,3,1,0:T(8,128)} %param.7, f32[1792,64]{0,1:T(8,128)} %param.9, s32[]{:T(128)S(6)} %select_n.3), kind=kOutput, calls=%fused_computation.5 | convolution fusion | flops 154370048 | bytes 1409028 | tf_op jit(solution)/shard_map/lij,jk->lik/dot_general | solution.py:25
  10.4 0.0 reduce-scatter.3.cloned.1.call-update
  10.4 0.0 reduce-scatter.5.cloned.1.call-start
  10.5 0.0 copy-done
  10.5 4.2 %fusion = bf16[8,1216,64]{1,2,0:T(8,128)(2,1)} fusion(f32[1,8,1216,56]{2,3,1,0:T(8,128)S(1)} %copy-done, f32[1792,64]{0,1:T(8,128)} %param.9, s32[]{:T(128)S(6)} %select_n.3), kind=kOutput, calls=%fused_computation.1 | convolution fusion | flops 419004416 | bytes 3457028 | tf_op jit(solution)/shard_map/lij,jk->lik/dot_general | solution.py:28
  14.7 0.0 reduce-scatter.5.cloned.1.call-update
  14.7 0.0 all-reduce.5.cloned.1.call-start
  14.8 27.6 %reduce-scatter.3.cloned.1.call-done = bf16[4,448,64]{1,2,0:T(8,128)(2,1)} async-done(((bf16[8,448,64]{1,2,0:T(8,128)(2,1)}), bf16[4,448,64]{1,2,0:T(8,128)(2,1)}) %reduce-scatter.3.cloned.1.call-update) | async-done | bytes 229392 | tf_op jit(solution)/shard_map/reduce_scatter | solution.py:32
  42.3 2.0 copy.35
  44.3 43.5 %reduce-scatter.5.cloned.1.call-done = bf16[4,1216,64]{1,2,0:T(8,128)(2,1)} async-done(((bf16[8,1216,64]{1,2,0:T(8,128)(2,1)}), bf16[4,1216,64]{1,2,0:T(8,128)(2,1)}) %reduce-scatter.5.cloned.1.call-update) | async-done | bytes 622608 | tf_op jit(solution)/shard_map/reduce_scatter | solution.py:35
  87.8 3.2 %copy.43 = bf16[4,1216,64]{2,0,1:T(4,128)(2,1)} copy(bf16[4,1216,64]{1,2,0:T(8,128)(2,1)} %reduce-scatter.5.cloned.1.call-done) | data formatting | bytes 1245184 | tf_op jit(solution)/shard_map/reduce_scatter | solution.py:35
  91.0 0.0 all-reduce.5.cloned.1.call-update
  91.1 0.0 all-gather.2.cloned.1.call-start
  91.1 0.6 copy-done.4
  91.7 0.6 dynamic-slice
  93.0 112.2 %all-reduce.5.cloned.1.call-done = (bf16[4,448,64]{2,0,1:T(4,128)(2,1)}, bf16[4,1216,64]{2,0,1:T(4,128)(2,1)}) async-done(((bf16[4,448,64]{2,0,1:T(4,128)(2,1)}, bf16[4,1216,64]{2,0,1:T(4,128)(2,1)}), (bf16[4,448,64]{2,0,1:T(4,128)(2,1)}, bf16[4,1216,64]{2,0,1:T(4,128)(2,1)})) %all-reduce.5.cloned.1.call-update) | async-done | bytes 851984
  205.2 0.8 convert_multiply_fusion
  205.9 4.2 %fusion.20 = (f32[4,1,38,1792]{3,2,0,1:T(8,128)}, bf16[4,38,1792]{2,1,0:T(8,128)(2,1)}, f32[4,1,38,1792]{3,2,0,1:T(8,128)S(1)}) fusion(f32[4,1,38,1792]{3,1,2,0:T(1,128)} %param.13, f32[4,1,38,1792]{3,1,2,0:T(1,128)} %param.11, f32[1792,64]{0,1:T(8,128)} %param.9, f32[4,38,64]{2,0,1:T(4,128)S(1)} %convert_multiply_fusion), kind=kOutput, calls=%fused_computation.32 | convolution fusion | flops 211097600 | bytes 5400576 | tf_op jit(solution)/shard_map/lik,jk->lij/dot_general | solution.py:12
  210.1 3.6 %copy.46 = bf16[4,38,1792]{1,0,2:T(4,128)(2,1)} copy(bf16[4,38,1792]{2,1,0:T(8,128)(2,1)} %get-tuple-element.27) | data formatting | bytes 1089536 | tf_op jit(solution)/shard_map/convert_element_type | solution.py:52
  213.7 5.8 %reshape.22 = bf16[32,2,4256]{2,1,0:T(2,128)(2,1)} reshape(bf16[1792,4,38]{2,1,0:T(4,128)(2,1)} %bitcast.82) | data formatting | bytes 1089536
  219.4 17.7 %all_to_all.36 = bf16[32,2,4256]{2,1,0:T(2,128)(2,1)} all-to-all(bf16[32,2,4256]{2,1,0:T(2,128)(2,1)} %reshape.22), channel_id=1, replica_groups=mesh['rep'=2,'fsdp'=32,'tp'=4] {'fsdp'}, dimensions={0} | all-to-all | bytes 1089536 | tf_op jit(solution)/shard_map/all_to_all | solution.py:55
  237.2 7.4 %reshape.23 = bf16[1792,4,38]{2,1,0:T(4,128)(2,1)} reshape(bf16[32,2,4256]{2,1,0:T(2,128)(2,1)} %all_to_all.36) | data formatting | bytes 1089536
  244.6 3.5 %copy.100 = bf16[4,38,32,56]{1,2,3,0:T(8,128)(2,1)} copy(bf16[4,38,32,56]{1,0,3,2:T(4,128)(2,1)} %bitcast.80) | data formatting | bytes 1089536 | tf_op jit(solution)/shard_map/all_to_all | solution.py:55
  248.0 4.7 %all_to_all.33 = bf16[4,1216,56]{1,2,0:T(8,128)(2,1)} reshape(bf16[4,32,38,56]{2,1,3,0:T(8,128)(2,1)} %bitcast.81) | data formatting | bytes 1089536 | tf_op jit(solution)/shard_map/all_to_all | solution.py:55
  252.7 0.0 all-gather.2.cloned.1.call-update
  253.4 0.0 copy-start.1
  253.4 1.2 copy.101
  254.5 0.7 convert_multiply_fusion.1
  255.3 2.6 fusion.18
  257.9 3.3 %copy.39 = bf16[4,14,1792]{1,0,2:T(4,128)(2,1)} copy(bf16[4,14,1792]{2,1,0:T(8,128)(2,1)} %get-tuple-element.30) | data formatting | bytes 401408 | tf_op jit(solution)/shard_map/convert_element_type | solution.py:51
  261.2 4.8 %reshape.20 = bf16[32,2,1568]{2,1,0:T(2,128)(2,1)} reshape(bf16[1792,4,14]{2,1,0:T(4,128)(2,1)} %bitcast.83) | data formatting | bytes 401408
  266.1 4.8 %all-to-all-start = ((bf16[32,2,1568]{2,1,0:T(2,128)(2,1)}), bf16[32,2,1568]{2,1,0:T(2,128)(2,1)}, u32[]{:S(2)}, u32[]{:S(2)}) async-start(bf16[32,2,1568]{2,1,0:T(2,128)(2,1)} %reshape.20), calls=%async_computation.1 | async-start | bytes 425984 | tf_op jit(solution)/shard_map/all_to_all | solution.py:54
  270.8 3.4 %copy.50 = f32[4,1,38,1792]{3,1,2,0:T(1,128)} copy(f32[4,1,38,1792]{3,2,0,1:T(8,128)} %get-tuple-element.26) | data formatting | bytes 2179072
  274.2 2.1 copy.52
  276.3 0.0 copy-done.3
  276.3 1.2 copy.49
  277.5 0.0 copy-done.2
  277.5 1.2 copy.51
  278.7 0.3 all-to-all-done
  279.0 6.8 %reshape.21 = bf16[1792,4,14]{2,1,0:T(4,128)(2,1)} reshape(bf16[32,2,1568]{2,1,0:T(2,128)(2,1)} %all-to-all-done) | data formatting | bytes 401408
  285.8 3.4 %copy.53 = bf16[4,14,32,56]{3,2,0,1:T(8,128)(2,1)S(1)} copy(bf16[4,14,32,56]{1,0,3,2:T(4,128)(2,1)} %bitcast.84) | data formatting | bytes 401408 | tf_op jit(solution)/shard_map/all_to_all | solution.py:54
  289.1 0.2 copy.41
  289.4 0.3 copy.42
  289.7 17.3 %all_gather.6 = bf16[8,448,56]{1,2,0:T(8,128)(2,1)S(1)} all-gather(bf16[4,448,56]{1,2,0:T(8,128)(2,1)S(1)} %copy.42), channel_id=1, replica_groups=mesh['rep'=2,'fsdp'=32,'tp'=4] {'rep'}, dimensions={0}, use_global_device_ids=true | all-gather | bytes 602112 | tf_op jit(solution)/shard_map/all_gather | solution.py:58
  307.0 0.8 copy.106
  307.8 2.3 copy.107
  (5 shorter events, 0.0 us)
Async XLA Ops:
  7.2 3.3 %copy-start = (f32[1,8,1216,56]{2,3,1,0:T(8,128)S(1)}, f32[1,8,1216,56]{2,3,1,0:T(8,128)}, u32[]{:S(2)}) copy-start(f32[1,8,1216,56]{2,3,1,0:T(8,128)} %param.8) | copy-start | bytes 6537220
  7.2 35.2 %reduce-scatter.3.cloned.1.call-start = ((), (), s32[]{:S(2)}) async-start(), calls=%async_computation.4 | async-start | bytes 786432 | tf_op jit(solution)/shard_map/reduce_scatter | solution.py:32
  10.4 77.4 %reduce-scatter.5.cloned.1.call-start = ((), (), s32[]{:S(2)}) async-start(), calls=%async_computation.5 | async-start | bytes 1966080 | tf_op jit(solution)/shard_map/reduce_scatter | solution.py:35
  14.7 190.4 %all-reduce.5.cloned.1.call-start = ((), (), s32[]{:S(2)}) async-start(), calls=%async_computation.7 | async-start | bytes 3407872
  91.0 0.7 copy-start.4
  91.1 215.9 %all-gather.2.cloned.1.call-start = ((), (), s32[]{:S(2)}) async-start(), calls=%async_computation.6 | async-start | bytes 1720320 | tf_op jit(solution)/shard_map/all_gather | solution.py:59
  253.4 1.9 copy-start.1
  266.1 12.9 %all-to-all-start = ((bf16[32,2,1568]{2,1,0:T(2,128)(2,1)}), bf16[32,2,1568]{2,1,0:T(2,128)(2,1)}, u32[]{:S(2)}, u32[]{:S(2)}) async-start(bf16[32,2,1568]{2,1,0:T(2,128)(2,1)} %reshape.20), calls=%async_computation.1 | async-start | bytes 425984 | tf_op jit(solution)/shard_map/all_to_all | solution.py:54
  274.2 2.1 copy-start.3
  274.2 3.3 %copy-start.2 = (f32[4,1,14,1792]{3,2,0,1:T(8,128)S(1)}, f32[4,1,14,1792]{3,2,0,1:T(8,128)}, u32[]{:S(2)}) copy-start(f32[4,1,14,1792]{3,2,0,1:T(8,128)} %get-tuple-element.31) | copy-start | bytes 1204228
Sparse Core Ops, SparseCore 0:
  11.1 31.2 reduce-scatter.2
  45.0 42.7 reduce-scatter.4
  91.8 113.3 all-reduce.4
  252.8 40.9 all-gather.1
where the time goes:
time: 318 us; the launch traced here: 317 us
  waiting for transfers between devices  184 us (58%)
  local copies, waits for them, and re-layouts  62.2 us (20%)
  blocking collectives  35 us (11%)
  between operations  15.2 us (5%)
  matrix products  14.1 us (4%)
  starting transfers between devices  4.95 us (2%)
    unnamed x5, waiting for transfers between devices  112 us
    reduce_scatter x1, waiting for transfers between devices, per_device(): lax.psum_scatter(partial_down.astype(jnp.bfloat16), 'rep', scatter_dimens...  43.5 us
    unnamed x22, local copies, waits for them, and re-layouts  38 us
    reduce_scatter x1, waiting for transfers between devices, per_device(): lax.psum_scatter(partial_out.astype(jnp.bfloat16), 'rep', scatter_dimensi...  27.6 us
    all_to_all x1, blocking collectives, per_device(): lax.all_to_all(rounded_down, 'fsdp', split_axis=2, concat_axis=1, tiled=T...  17.7 us
    all_gather x1, blocking collectives, per_device(): lax.all_gather(placed_out, 'rep', axis=0, tiled=True)  17.3 us
    all_to_all x2, local copies, waits for them, and re-layouts, per_device(): lax.all_to_all(rounded_down, 'fsdp', split_axis=2, concat_axis=1, tiled=T...  8.1 us
    dot_general x2, matrix products, owner_update(): jnp.einsum('lik,jk->lij', coef, basis, precision=lax.Precision.HIGHEST)  6.77 us
  transfers between devices with their start and end apart: 5, of which 4 were waited for; matrix products, arithmetic and copies ran while one was open for 12% of the time, Pallas kernels for 0%

commit v1 on v0

--- a/solution.py
+++ b/solution.py
@@ -55,7 +55,9 @@
         lax.all_to_all(rounded_down, "fsdp", split_axis=2, concat_axis=1, tiled=True),
     )
     weights_out, weights_down = (
-        lax.all_gather(placed_out, "rep", axis=0, tiled=True),
+        jnp.concatenate(
+            lax.all_to_all(jnp.stack([placed_out] * lax.axis_size("rep")), "rep", 0, 0), axis=0
+        ),
         lax.all_gather(placed_down, "rep", axis=0, tiled=True),
     )
     return (

time: 318 us -> 328 us (1.031)
  blocking collectives: 35 us -> 12.9 us
  waiting for transfers between devices: 184 us -> 202 us
  starting transfers between devices: 4.95 us -> 12 us
  local copies, waits for them, and re-layouts: 62.2 us -> 67.6 us
    all_to_all x1 -> x2, waiting for transfers between devices: 0.34 us -> 18.2 us  [the longest x1 9.41 us: per_device(): lax.all_to_all(rounded_down, 'fsdp', split_axis=2, concat_axis=1, tiled=T...]
    all_gather x1 -> x0, blocking collectives: 17.3 us -> none  [per_device(): lax.all_gather(placed_out, 'rep', axis=0, tiled=True)]
    all_to_all x1 -> x2, starting transfers between devices: 4.79 us -> 11.7 us  [the longest x1 6.1 us: per_device(): lax.all_to_all(jnp.stack([placed_out] * lax.axis_size('rep')), 'rep', 0, 0)]
    all_to_all x1, blocking collectives: 17.7 us -> 12.9 us  [per_device(): lax.all_to_all(rounded_out, 'fsdp', split_axis=2, concat_axis=1, tiled=True)]
    unnamed x22 -> x20, local copies, waits for them, and re-layouts: 38 us -> 39.8 us
  transfers between devices with their start and end apart: 5 -> 6, of which waited for: 4 -> 5; matrix products, arithmetic and copies ran while one was open for 12% -> 13% of each run, Pallas kernels for 0% -> 0%
where the time goes in v1:
time: 328 us; the launch traced here: 326 us
  waiting for transfers between devices  202 us (62%)
  local copies, waits for them, and re-layouts  67.6 us (21%)
  between operations  15.1 us (5%)
  matrix products  14.4 us (4%)
  blocking collectives  12.9 us (4%)
  starting transfers between devices  12 us (4%)
    unnamed x5, waiting for transfers between devices  112 us
    reduce_scatter x1, waiting for transfers between devices, per_device(): lax.psum_scatter(partial_down.astype(jnp.bfloat16), 'rep', scatter_dimens...  43.5 us
    unnamed x20, local copies, waits for them, and re-layouts  39.8 us
    reduce_scatter x1, waiting for transfers between devices, per_device(): lax.psum_scatter(partial_out.astype(jnp.bfloat16), 'rep', scatter_dimensi...  27.6 us
    all_to_all x1, blocking collectives, per_device(): lax.all_to_all(rounded_out, 'fsdp', split_axis=2, concat_axis=1, tiled=True)  12.9 us
    all_to_all x1, waiting for transfers between devices, per_device(): lax.all_to_all(rounded_down, 'fsdp', split_axis=2, concat_axis=1, tiled=T...  9.41 us
    all_to_all x1, waiting for transfers between devices, per_device(): lax.all_to_all(jnp.stack([placed_out] * lax.axis_size('rep')), 'rep', 0, 0)  8.78 us
    all_to_all x2, local copies, waits for them, and re-layouts, per_device(): lax.all_to_all(rounded_down, 'fsdp', split_axis=2, concat_axis=1, tiled=T...  8.09 us
  transfers between devices with their start and end apart: 6, of which 5 were waited for; matrix products, arithmetic and copies ran while one was open for 13% of the time, Pallas kernels for 0%

profile of v1, /device:TPU:32, one launch (start us, length us, event | category | flops | bytes accessed | tf_op | source)
XLA Modules:
  0.0 326.5 jit_solution(10697939920983522356)
XLA Ops:
  7.2 0.0 copy-start
  7.2 0.0 reduce-scatter.3.cloned.1.call-start
  7.2 3.2 fusion.2
  10.4 0.0 reduce-scatter.3.cloned.1.call-update
  10.4 0.0 reduce-scatter.5.cloned.1.call-start
  10.5 0.0 copy-done
  10.5 4.2 %fusion = bf16[8,1216,64]{1,2,0:T(8,128)(2,1)} fusion(f32[1,8,1216,56]{2,3,1,0:T(8,128)S(1)} %copy-done, f32[1792,64]{0,1:T(8,128)} %param.9, s32[]{:T(128)S(6)} %select_n.3), kind=kOutput, calls=%fused_computation.1 | convolution fusion | flops 419004416 | bytes 3457028 | tf_op jit(solution)/shard_map/lij,jk->lik/dot_general | solution.py:28
  14.7 0.0 reduce-scatter.5.cloned.1.call-update
  14.7 0.0 all-reduce.5.cloned.1.call-start
  14.8 27.6 %reduce-scatter.3.cloned.1.call-done = bf16[4,448,64]{1,2,0:T(8,128)(2,1)} async-done(((bf16[8,448,64]{1,2,0:T(8,128)(2,1)}), bf16[4,448,64]{1,2,0:T(8,128)(2,1)}) %reduce-scatter.3.cloned.1.call-update) | async-done | bytes 229392 | tf_op jit(solution)/shard_map/reduce_scatter | solution.py:32
  42.3 2.0 copy.48
  44.3 43.5 %reduce-scatter.5.cloned.1.call-done = bf16[4,1216,64]{1,2,0:T(8,128)(2,1)} async-done(((bf16[8,1216,64]{1,2,0:T(8,128)(2,1)}), bf16[4,1216,64]{1,2,0:T(8,128)(2,1)}) %reduce-scatter.5.cloned.1.call-update) | async-done | bytes 622608 | tf_op jit(solution)/shard_map/reduce_scatter | solution.py:35
  87.8 3.2 copy.56
  91.0 0.0 all-reduce.5.cloned.1.call-update
  91.1 0.6 copy-done.3
  91.7 0.6 dynamic-slice
  92.9 112.2 %all-reduce.5.cloned.1.call-done = (bf16[4,448,64]{2,0,1:T(4,128)(2,1)}, bf16[4,1216,64]{2,0,1:T(4,128)(2,1)}) async-done(((bf16[4,448,64]{2,0,1:T(4,128)(2,1)}, bf16[4,1216,64]{2,0,1:T(4,128)(2,1)}), (bf16[4,448,64]{2,0,1:T(4,128)(2,1)}, bf16[4,1216,64]{2,0,1:T(4,128)(2,1)})) %all-reduce.5.cloned.1.call-update) | async-done | bytes 851984
  205.2 0.8 convert_multiply_fusion
  205.9 4.2 %fusion.20 = (f32[4,1,38,1792]{3,2,0,1:T(8,128)}, bf16[4,38,1792]{2,1,0:T(8,128)(2,1)}, f32[4,1,38,1792]{3,2,0,1:T(8,128)S(1)}) fusion(f32[4,1,38,1792]{3,1,2,0:T(1,128)} %param.13, f32[4,1,38,1792]{3,1,2,0:T(1,128)} %param.11, f32[1792,64]{0,1:T(8,128)} %param.9, f32[4,38,64]{2,0,1:T(4,128)S(1)} %convert_multiply_fusion), kind=kOutput, calls=%fused_computation.33 | convolution fusion | flops 211097600 | bytes 5400576 | tf_op jit(solution)/shard_map/lik,jk->lij/dot_general | solution.py:12
  210.1 3.6 %copy.59 = bf16[4,38,1792]{1,0,2:T(4,128)(2,1)} copy(bf16[4,38,1792]{2,1,0:T(8,128)(2,1)} %get-tuple-element.33) | data formatting | bytes 1089536 | tf_op jit(solution)/shard_map/convert_element_type | solution.py:52
  213.7 5.8 %reshape.27 = bf16[32,2,4256]{2,1,0:T(2,128)(2,1)} reshape(bf16[1792,4,38]{2,1,0:T(4,128)(2,1)} %bitcast.83) | data formatting | bytes 1089536
  219.4 5.6 %all-to-all-start.2 = ((bf16[32,2,4256]{2,1,0:T(2,128)(2,1)}), bf16[32,2,4256]{2,1,0:T(2,128)(2,1)}, u32[]{:S(2)}, u32[]{:S(2)}) async-start(bf16[32,2,4256]{2,1,0:T(2,128)(2,1)} %reshape.27), calls=%async_computation.4 | async-start | bytes 1114112 | tf_op jit(solution)/shard_map/all_to_all | solution.py:55
  225.0 0.2 all-gather.2.cloned.1.call-start
  225.9 1.9 copy.114
  227.8 9.4 %all-to-all-done.2 = bf16[32,2,4256]{2,1,0:T(2,128)(2,1)} async-done(((bf16[32,2,4256]{2,1,0:T(2,128)(2,1)}), bf16[32,2,4256]{2,1,0:T(2,128)(2,1)}, u32[]{:S(2)}, u32[]{:S(2)}) %all-to-all-start.2) | async-done | bytes 544800 | tf_op jit(solution)/shard_map/all_to_all | solution.py:55
  237.2 7.4 %reshape.28 = bf16[1792,4,38]{2,1,0:T(4,128)(2,1)} reshape(bf16[32,2,4256]{2,1,0:T(2,128)(2,1)} %all-to-all-done.2) | data formatting | bytes 1089536
  244.6 3.4 %copy.113 = bf16[4,38,32,56]{1,2,3,0:T(8,128)(2,1)} copy(bf16[4,38,32,56]{1,0,3,2:T(4,128)(2,1)} %bitcast.81) | data formatting | bytes 1089536 | tf_op jit(solution)/shard_map/all_to_all | solution.py:55
  248.0 4.6 %all_to_all.34 = bf16[4,1216,56]{1,2,0:T(8,128)(2,1)} reshape(bf16[4,32,38,56]{2,1,3,0:T(8,128)(2,1)} %bitcast.82) | data formatting | bytes 1089536 | tf_op jit(solution)/shard_map/all_to_all | solution.py:55
  252.7 0.0 all-gather.2.cloned.1.call-update
  252.7 0.7 convert_multiply_fusion.1
  253.4 2.9 fusion.18
  256.3 3.3 %copy.52 = bf16[4,14,1792]{1,0,2:T(4,128)(2,1)} copy(bf16[4,14,1792]{2,1,0:T(8,128)(2,1)} %get-tuple-element.36) | data formatting | bytes 401408 | tf_op jit(solution)/shard_map/convert_element_type | solution.py:51
  259.6 4.8 %reshape.25 = bf16[32,2,1568]{2,1,0:T(2,128)(2,1)} reshape(bf16[1792,4,14]{2,1,0:T(4,128)(2,1)} %bitcast.84) | data formatting | bytes 401408
  264.4 12.9 %all_to_all.38 = bf16[32,2,1568]{2,1,0:T(2,128)(2,1)} all-to-all(bf16[32,2,1568]{2,1,0:T(2,128)(2,1)} %reshape.25), channel_id=1, replica_groups=mesh['rep'=2,'fsdp'=32,'tp'=4] {'fsdp'}, dimensions={0} | all-to-all | bytes 401408 | tf_op jit(solution)/shard_map/all_to_all | solution.py:54
  277.3 6.8 %reshape.26 = bf16[1792,4,14]{2,1,0:T(4,128)(2,1)} reshape(bf16[32,2,1568]{2,1,0:T(2,128)(2,1)} %all_to_all.38) | data formatting | bytes 401408
  284.1 4.2 %copy.66 = bf16[4,14,32,56]{3,2,0,1:T(8,128)(2,1)} copy(bf16[4,14,32,56]{1,0,3,2:T(4,128)(2,1)} %bitcast.85) | data formatting | bytes 401408 | tf_op jit(solution)/shard_map/all_to_all | solution.py:54
  288.2 1.3 copy.54
  289.5 1.4 pad_maximum_fusion
  290.9 2.2 copy.55
  293.1 6.1 %all-to-all-start.1 = ((bf16[2,4,448,56]{2,3,1,0:T(8,128)(2,1)}), bf16[2,4,448,56]{2,3,1,0:T(8,128)(2,1)}, u32[]{:S(2)}, u32[]{:S(2)}) async-start(bf16[2,4,448,56]{2,3,1,0:T(8,128)(2,1)} %copy.55), calls=%async_computation.2 | async-start | bytes 917504 | tf_op jit(solution)/shard_map/all_to_all | solution.py:59
  299.2 3.4 %copy.63 = f32[4,1,38,1792]{3,1,2,0:T(1,128)} copy(f32[4,1,38,1792]{3,2,0,1:T(8,128)} %get-tuple-element.32) | data formatting | bytes 2179072
  302.5 2.1 copy.65
  304.7 0.0 copy-done.2
  304.7 1.2 copy.62
  305.8 1.2 copy.64
  307.0 8.8 %all-to-all-done.1 = bf16[2,4,448,56]{2,3,1,0:T(8,128)(2,1)} async-done(((bf16[2,4,448,56]{2,3,1,0:T(8,128)(2,1)}), bf16[2,4,448,56]{2,3,1,0:T(8,128)(2,1)}, u32[]{:S(2)}, u32[]{:S(2)}) %all-to-all-start.1) | async-done | bytes 401440 | tf_op jit(solution)/shard_map/all_to_all | solution.py:59
  315.8 1.8 copy.119
  317.6 2.3 copy.120
  (5 shorter events, 0.0 us)
Async XLA Ops:
  7.2 3.3 %copy-start = (f32[1,8,1216,56]{2,3,1,0:T(8,128)S(1)}, f32[1,8,1216,56]{2,3,1,0:T(8,128)}, u32[]{:S(2)}) copy-start(f32[1,8,1216,56]{2,3,1,0:T(8,128)} %param.8) | copy-start | bytes 6537220
  7.2 35.2 %reduce-scatter.3.cloned.1.call-start = ((), (), s32[]{:S(2)}) async-start(), calls=%async_computation.5 | async-start | bytes 786432 | tf_op jit(solution)/shard_map/reduce_scatter | solution.py:32
  10.4 77.4 %reduce-scatter.5.cloned.1.call-start = ((), (), s32[]{:S(2)}) async-start(), calls=%async_computation.6 | async-start | bytes 1966080 | tf_op jit(solution)/shard_map/reduce_scatter | solution.py:35
  14.7 190.4 %all-reduce.5.cloned.1.call-start = ((), (), s32[]{:S(2)}) async-start(), calls=%async_computation.8 | async-start | bytes 3407872
  91.0 0.7 copy-start.3
  219.4 17.7 %all-to-all-start.2 = ((bf16[32,2,4256]{2,1,0:T(2,128)(2,1)}), bf16[32,2,4256]{2,1,0:T(2,128)(2,1)}, u32[]{:S(2)}, u32[]{:S(2)}) async-start(bf16[32,2,4256]{2,1,0:T(2,128)(2,1)} %reshape.27), calls=%async_computation.4 | async-start | bytes 1114112 | tf_op jit(solution)/shard_map/all_to_all | solution.py:55
  225.0 90.7 %all-gather.2.cloned.1.call-start = ((), (), s32[]{:S(2)}) async-start(), calls=%async_computation.7 | async-start | bytes 1720320 | tf_op jit(solution)/shard_map/all_gather | solution.py:61
  293.1 22.7 %all-to-all-start.1 = ((bf16[2,4,448,56]{2,3,1,0:T(8,128)(2,1)}), bf16[2,4,448,56]{2,3,1,0:T(8,128)(2,1)}, u32[]{:S(2)}, u32[]{:S(2)}) async-start(bf16[2,4,448,56]{2,3,1,0:T(8,128)(2,1)} %copy.55), calls=%async_computation.2 | async-start | bytes 917504 | tf_op jit(solution)/shard_map/all_to_all | solution.py:59
  302.5 2.1 copy-start.2
  302.5 3.3 %copy-start.1 = (f32[4,1,14,1792]{3,2,0,1:T(8,128)S(1)}, f32[4,1,14,1792]{3,2,0,1:T(8,128)}, u32[]{:S(2)}) copy-start(f32[4,1,14,1792]{3,2,0,1:T(8,128)} %get-tuple-element.37) | copy-start | bytes 1204228
Sparse Core Ops, SparseCore 0:
  11.1 31.2 reduce-scatter.2
  45.0 42.7 reduce-scatter.4
  91.8 113.3 all-reduce.4
  252.8 40.9 all-gather.1
